TPU v7x, 128 devices: a whole 4x4x4 slice. The times are simulated.
128 devices in a mesh: mem: 8 (over y_hi, x), dom: 16 (over z, y_lo, core).
Axes of the slice: x: 4, y: 4 (y_hi: 2, y_lo: 2; y = y_hi * 2 + y_lo), z: 4, core: 2. Of those that a mesh axis runs over, the one named last changes fastest.
Arguments:
- sample_vectors_prior: float32 [32, 5, 512, 256], P('mem', None, 'dom'), may hold values from -6 to 6
- smoothing_number: float32 [5, 512, 256], P(None, 'dom'), may hold values from 0.02 to 0.2
- cross_quantity_factor: float32 [5, 5], replicated, may hold values from -0.6 to 0.6
- obs_tile: int32 [2, 2048, 1], replicated, may hold values from 0 to 15; in each aligned block of 2048 rows (0 to 2047, 2048 to 4095, ..., all dimensions but the last counted through in order) at most 256 rows name the same one
- measured_gridpoint: int32 [2, 2048], replicated, may hold values from 0 to 7904
- obs_field: int32 [2, 2048], replicated, may hold values from 0 to 4
- obs_weights: float32 [2, 2048, 4], replicated, may hold values from 0.1 to 0.5
- obs_values: float32 [2, 2048], replicated, may hold values from -8 to 8
- observation_variance: float32 [2, 2048], replicated, may hold values from 0.2 to 2
- localization: float32 [2, 16, 2048], P(None, 'dom'), may hold values from 0.001 to 0.02
Outputs:
- analysis: float32 [32, 5, 512, 256], P('mem', None, 'dom')
Inputs may be any that keep to these rules, and one draw needn't show every extreme that they name: `obs_tile`: in each batch at most 256 observations share an owning tile, and in some batch some tile owns exactly 256. Local row measured_gridpoint // 255, column measured_gridpoint % 255; the four points used lie in the owning tile.
All inputs are finite; a program needn't handle non-finite values.
Results may differ from a plain program's by a relative error of at most 0.0001.
Values sent between devices are 32-bit elements; how exact they have to be, the bound alone decides.
No kernel may reach another device: no remote copies, remote signals or barrier semaphores. Data moves between devices by JAX's collectives and lax.ppermute only.
A program may use at most 128 MiB of HBM per device.

v0:
```python
import jax
import jax.numpy as jnp
from jax import lax
from jax.sharding import PartitionSpec as P

STEPS = 2


def with_halo(cells, sides, width):
    for axis, dim in sides:
        count = lax.axis_size(axis)
        ends = count - 1
        head = lax.slice_in_dim(cells, 0, width, axis=dim)
        tail = lax.slice_in_dim(cells, cells.shape[dim] - width, cells.shape[dim], axis=dim)
        cells = jnp.concatenate(
            [
                lax.ppermute(tail, axis, [(i, (i + 1) % count) for i in range(ends)]),
                cells,
                lax.ppermute(head, axis, [((i + 1) % count, i) for i in range(ends)]),
            ],
            axis=dim,
        )
    return cells


def predicted_quantity(sample_vectors_prior, smoothing_number, cross_quantity_factor):
    padded = with_halo(sample_vectors_prior, (("dom", 2),), 1)
    padded = jnp.pad(padded, ((0, 0), (0, 0), (0, 0), (1, 1)))
    lap = padded[:, :, 2:, 1:-1] + padded[:, :, :-2, 1:-1]
    lap = lap + padded[:, :, 1:-1, 2:] + padded[:, :, 1:-1, :-2] - 4.0 * sample_vectors_prior
    mixed = jnp.einsum(
        "fg,mgxy->mfxy",
        cross_quantity_factor,
        sample_vectors_prior,
        precision=lax.Precision.HIGHEST,
    )
    return sample_vectors_prior + smoothing_number[None] * lap + mixed


def local_priors(
    sample_vectors_prior, obs_tile, measured_gridpoint, obs_field, obs_weights, batch_index, my_tile
):
    sample_total_size, fields, tile_row_count, columns = sample_vectors_prior.shape
    nobs_count = measured_gridpoint.shape[1]
    offsets = jnp.array([0, 1, columns, columns + 1], dtype=jnp.int32)
    owner = obs_tile[batch_index, :, 0]
    place = measured_gridpoint[batch_index]
    base = (
        obs_field[batch_index] * (tile_row_count * columns)
        + place // (columns - 1) * columns
        + place % (columns - 1)
    )
    points = (base[:, None] + offsets[None, :]).reshape(-1)
    flat = sample_vectors_prior.reshape(sample_total_size, fields * tile_row_count * columns)
    values = jnp.take(flat, points, axis=1).reshape(sample_total_size, nobs_count, 4)
    local_prior = jnp.sum(values * obs_weights[batch_index][None], axis=-1)
    owned_mask = owner == my_tile
    return (local_prior, owner, owned_mask)


def share_priors(local_prior, owned_mask):
    masked = jnp.where(owned_mask[None], local_prior, jnp.float32(0.0))
    summed = lax.psum(masked, "dom")
    prior = lax.all_gather(summed, "mem", axis=0, tiled=True)
    return prior


def batch_mixing(prior, obs_values, observation_variance, localization, batch_index):
    members = prior.shape[0]
    mean_prior = jnp.mean(prior, axis=0)
    ensemble_spread = prior - mean_prior[None]
    variance = jnp.sum(ensemble_spread * ensemble_spread, axis=0) / (members - 1)
    error = observation_variance[batch_index]
    total = variance + error
    gain = (obs_values[batch_index] - mean_prior)[None] / total[None] - ensemble_spread / (
        jnp.sqrt(total) * (jnp.sqrt(error) + jnp.sqrt(total))
    )[None]
    return jnp.einsum(
        "mo,to,no->tmn",
        ensemble_spread,
        localization[batch_index],
        gain,
        precision=lax.Precision.HIGHEST,
    )[0] / (members - 1)


def apply_update(sample_vectors_prior, mixing):
    sample_total_size, fields, tile_row_count, columns = sample_vectors_prior.shape
    members = sample_total_size * lax.axis_size("mem")
    flat = sample_vectors_prior.reshape(sample_total_size, fields * tile_row_count * columns)
    own_columns = lax.dynamic_slice_in_dim(
        mixing, lax.axis_index("mem") * sample_total_size, sample_total_size, 1
    )
    piece = lax.all_gather(flat, "mem", axis=0, tiled=True)
    product = jnp.dot(
        own_columns.T, piece, precision=lax.Precision.HIGHEST, preferred_element_type=jnp.float32
    )
    member_total = jnp.sum(piece, axis=0)
    average = member_total / members
    updated = flat + product - jnp.sum(own_columns, axis=0)[:, None] * average[None]
    return updated.reshape(sample_total_size, fields, tile_row_count, columns)


def on_device(
    sample_vectors_prior,
    smoothing_number,
    cross_quantity_factor,
    obs_tile,
    measured_gridpoint,
    obs_field,
    obs_weights,
    obs_values,
    observation_variance,
    localization,
):
    my_tile = lax.axis_index("dom")
    for step_index in range(STEPS):
        sample_vectors_prior = predicted_quantity(
            sample_vectors_prior, smoothing_number, cross_quantity_factor
        )
    batch_count = obs_values.shape[0]
    for batch_index in range(batch_count):
        local_prior, owner, owned_mask = local_priors(
            sample_vectors_prior,
            obs_tile,
            measured_gridpoint,
            obs_field,
            obs_weights,
            batch_index,
            my_tile,
        )
        prior = share_priors(local_prior, owned_mask)
        mixing = batch_mixing(prior, obs_values, observation_variance, localization, batch_index)
        sample_vectors_prior = apply_update(sample_vectors_prior, mixing)
    return sample_vectors_prior


def solution(mesh):
    placed = (
        P("mem", None, "dom", None),
        P(None, "dom", None),
        P(),
        P(),
        P(),
        P(),
        P(),
        P(),
        P(),
        P(None, "dom", None),
    )
    return jax.shard_map(
        on_device,
        mesh=mesh,
        in_specs=placed,
        out_specs=P("mem", None, "dom", None),
        check_vma=False,
    )
```

profile of v0, /device:TPU:0, one launch (start us, length us, event | category | flops | bytes accessed | tf_op | source)
XLA Modules:
  0.0 404.2 jit_solution(9559365138855716027)
XLA Ops:
  6.5 1.5 copy.48
  8.1 1.3 collective-permute-start
  9.4 3.0 collective-permute-start.1
  12.4 1.0 copy.41
  13.4 0.5 select_maximum_fusion.2
  14.0 1.4 fusion.4
  15.3 1.3 collective-permute-start.2
  16.6 3.8 collective-permute-start.3
  20.5 0.8 collective-permute-done.3
  21.3 0.5 select_maximum_fusion
  21.8 1.4 fusion.3
  23.2 0.2 copy.50
  23.4 1.2 reshape.217
  24.9 0.6 broadcast_add_fusion
  25.5 0.6 add.178
  26.2 0.4 copy.52
  26.7 0.4 copy.59
  27.1 10.0 %copy.51 = f32[4,40960]{0,1:T(8,128)} copy(f32[4,40960]{1,0:T(4,128)S(1)} %bitcast.60) | data formatting | bytes 1310720 | tf_op jit(solution)/shard_map/reshape | solution.py:90
  37.1 35.3 %gather_fusion = f32[8192,4]{1,0:T(8,128)} fusion(f32[4,40960]{0,1:T(8,128)} %copy.51, s32[8192]{0:T(1024)S(1)} %fusion.31), kind=kCustom, calls=%fused_computation.clone | custom fusion | bytes 294912 | tf_op jit(solution)/shard_map/jit(_take)/gather | solution.py:55
  72.4 6.2 %broadcast_select_fusion.1 = f32[8192,4]{1,0:T(8,128)S(1)} fusion(f32[8192,4]{1,0:T(8,128)} %gather_fusion, pred[8192]{0:T(1024)(128)(4,1)S(1)} %compare_and_fusion.1), kind=kLoop, calls=%fused_computation.11 | loop fusion | flops 32768 | bytes 270336 | tf_op jit(solution)/shard_map/jit(_take)/select_n | solution.py:55
  78.6 11.2 %multiply_reduce_fusion.1 = f32[4,2048]{0,1:T(8,128)S(1)} fusion(f32[4,2048,4]{0,2,1:T(4,128)S(1)} %bitcast.56, f32[2048,4]{1,0:T(8,128)S(1)} %copy.52), kind=kLoop, calls=%fused_computation.7 | loop fusion | flops 57344 | bytes 196608 | tf_op jit(solution)/shard_map/reduce_sum | solution.py:56
  89.8 0.3 broadcast_select_fusion.3
  90.2 72.1 %psum.14 = f32[4,2048]{0,1:T(8,128)} all-reduce(f32[4,2048]{0,1:T(8,128)S(1)} %broadcast_select_fusion.3), channel_id=1, replica_groups=mesh['mem'=8,'dom'=16] {'dom'}, use_global_device_ids=true, to_apply=%region_1.3 | all-reduce | flops 8192 | bytes 65536 | tf_op jit(solution)/shard_map/psum | solution.py:63
  162.3 1.6 copy.53
  163.9 35.0 %all-gather = f32[8,4,2048]{2,1,0:T(4,128)S(1)} all-gather(f32[1,4,2048]{2,1,0:T(4,128)S(1)} %copy.53), channel_id=1, replica_groups=mesh['mem'=8,'dom'=16] {'mem'}, dimensions={0}, use_global_device_ids=true | all-gather | bytes 294912 | tf_op jit(solution)/shard_map/all_gather | solution.py:64
  198.8 0.1 reshape.216
  199.2 0.4 fusion.17
  199.5 0.1 fusion.41
  199.7 3.5 reduce_sum.94
  203.2 6.0 %reshape.218 = f32[32,40960]{1,0:T(8,128)} reshape(f32[8,4,40960]{2,1,0:T(4,128)} %all-gather.7.cloned.1.call-done) | data formatting | bytes 10485760
  209.2 6.0 %fusion.1 = f32[4,40960]{1,0:T(4,128)} fusion(f32[4,40960]{1,0:T(4,128)S(1)} %bitcast.61, f32[32,40960]{1,0:T(8,128)} %reshape.218, f32[40960]{0:T(1024)S(1)} %broadcast_multiply_fusion.1, f32[4]{0:T(128)S(1)} %fusion.41, f32[32,32]{0,1:T(8,128)S(1)} %fusion.17, s32[]{:T(128)S(6)} %select_n.56), kind=kOutput, calls=%fused_computation.5 | convolution fusion | flops 63406208 | bytes 6720004 | tf_op jit(solution)/shard_map/dot_general | solution.py:95
  215.2 0.6 add.189
  215.8 0.4 copy.56
  216.2 11.0 %copy.55 = f32[4,40960]{0,1:T(8,128)} copy(f32[4,40960]{1,0:T(4,128)} %fusion.1) | data formatting | bytes 1310720 | tf_op jit(solution)/shard_map/sub | solution.py:100
  227.2 34.7 %gather_fusion.1 = f32[8192,4]{1,0:T(8,128)} fusion(f32[4,40960]{0,1:T(8,128)} %copy.55, s32[8192]{0:T(1024)S(1)} %fusion.32), kind=kCustom, calls=%fused_computation.1.clone | custom fusion | bytes 294912 | tf_op jit(solution)/shard_map/jit(_take)/gather | solution.py:55
  261.9 6.2 %broadcast_select_fusion = f32[8192,4]{1,0:T(8,128)S(1)} fusion(f32[8192,4]{1,0:T(8,128)} %gather_fusion.1, pred[8192]{0:T(1024)(128)(4,1)S(1)} %compare_and_fusion), kind=kLoop, calls=%fused_computation.10 | loop fusion | flops 32768 | bytes 270336 | tf_op jit(solution)/shard_map/jit(_take)/select_n | solution.py:55
  268.2 11.2 %multiply_reduce_fusion = f32[4,2048]{0,1:T(8,128)S(1)} fusion(f32[4,2048,4]{0,2,1:T(4,128)S(1)} %bitcast.57, f32[2048,4]{1,0:T(8,128)S(1)} %copy.56), kind=kLoop, calls=%fused_computation.6 | loop fusion | flops 57344 | bytes 196608 | tf_op jit(solution)/shard_map/reduce_sum | solution.py:56
  279.4 0.3 broadcast_select_fusion.2
  279.7 66.1 %psum.15 = f32[4,2048]{0,1:T(8,128)S(1)} all-reduce(f32[4,2048]{0,1:T(8,128)S(1)} %broadcast_select_fusion.2), channel_id=1, replica_groups=mesh['mem'=8,'dom'=16] {'dom'}, use_global_device_ids=true, to_apply=%region_7.9 | all-reduce | flops 8192 | bytes 65536 | tf_op jit(solution)/shard_map/psum | solution.py:63
  345.9 0.3 copy.57
  346.2 34.7 %all-gather.2 = f32[8,4,2048]{2,1,0:T(4,128)S(1)} all-gather(f32[1,4,2048]{2,1,0:T(4,128)S(1)} %copy.57), channel_id=1, replica_groups=mesh['mem'=8,'dom'=16] {'mem'}, dimensions={0}, use_global_device_ids=true | all-gather | bytes 294912 | tf_op jit(solution)/shard_map/all_gather | solution.py:64
  380.9 0.1 reshape.220
  381.2 0.4 fusion.13
  381.6 0.1 fusion.42
  381.7 3.5 reduce_sum.99
  385.2 6.1 %reshape.222 = f32[32,40960]{1,0:T(8,128)} reshape(f32[8,4,40960]{2,1,0:T(4,128)} %all-gather.9.cloned.1.call-done) | data formatting | bytes 10485760
  391.3 5.1 %fusion = f32[4,40960]{1,0:T(4,128)S(1)} fusion(f32[4,40960]{1,0:T(4,128)S(1)} %copy-done.2, f32[32,40960]{1,0:T(8,128)} %reshape.222, f32[40960]{0:T(1024)S(1)} %broadcast_multiply_fusion, f32[4]{0:T(128)S(1)} %fusion.42, f32[32,32]{0,1:T(8,128)S(1)} %fusion.13, s32[]{:T(128)S(6)} %select_n.56), kind=kOutput, calls=%fused_computation.3 | convolution fusion | flops 63406208 | bytes 6720004 | tf_op jit(solution)/shard_map/dot_general | solution.py:95
  396.4 1.0 copy.60
  (56 shorter events, 0.8 us)
Async XLA Ops:
  6.5 7.4 %copy-start = (f32[5,5]{1,0:T(8,128)S(1)}, f32[5,5]{1,0:T(8,128)}, u32[]{:S(2)}) copy-start(f32[5,5]{1,0:T(8,128)} %param.16) | copy-start | bytes 304
  6.5 193.1 %all-gather.7.cloned.1.call-start = ((), (), s32[]{:S(2)}) async-start(), calls=%async_computation | async-start | bytes 5898240 | tf_op jit(solution)/shard_map/all_gather | solution.py:94
  8.1 5.4 %collective-permute-start = (f32[4,5,1,256]{3,1,2,0:T(8,128)S(1)}, f32[4,5,1,256]{3,1,2,0:T(8,128)S(1)}, u32[]{:S(2)}, u32[]{:S(2)}) collective-permute-start(f32[4,5,1,256]{3,1,2,0:T(8,128)S(1)} %get-tuple-element.13), channel_id=1, source_target_pairs={{1,0},{2,1},{3,2},{4,3},{5,4},{6,5},{7,6},{8,7},{9,8},{10,9},{11,1... | collective-permute-start | bytes 61448 | tf_op jit(solution)/shard_map/ppermute | solution.py:19
  9.4 4.1 %collective-permute-start.1 = (f32[4,5,1,256]{3,1,2,0:T(8,128)S(1)}, f32[4,5,1,256]{3,1,2,0:T(8,128)S(1)}, u32[]{:S(2)}, u32[]{:S(2)}) collective-permute-start(f32[4,5,1,256]{3,1,2,0:T(8,128)S(1)} %get-tuple-element.12), channel_id=1, source_target_pairs={{0,1},{1,2},{2,3},{3,4},{4,5},{5,6},{6,7},{7,8},{8,9},{9,10},{10,1... | collective-permute-start | bytes 61448 | tf_op jit(solution)/shard_map/ppermute | solution.py:17
  15.3 5.1 %collective-permute-start.2 = (f32[4,5,1,256]{3,1,2,0:T(8,128)S(1)}, f32[4,5,1,256]{3,1,2,0:T(8,128)S(1)}, u32[]{:S(2)}, u32[]{:S(2)}) collective-permute-start(f32[4,5,1,256]{3,1,2,0:T(8,128)S(1)} %get-tuple-element.11), channel_id=1, source_target_pairs={{1,0},{2,1},{3,2},{4,3},{5,4},{6,5},{7,6},{8,7},{9,8},{10,9},{11,1... | collective-permute-start | bytes 61448 | tf_op jit(solution)/shard_map/ppermute | solution.py:19
  16.6 4.7 %collective-permute-start.3 = (f32[4,5,1,256]{3,1,2,0:T(8,128)S(1)}, f32[4,5,1,256]{3,1,2,0:T(8,128)S(1)}, u32[]{:S(2)}, u32[]{:S(2)}) collective-permute-start(f32[4,5,1,256]{3,1,2,0:T(8,128)S(1)} %get-tuple-element.10), channel_id=1, source_target_pairs={{0,1},{1,2},{2,3},{3,4},{4,5},{5,6},{6,7},{7,8},{8,9},{9,10},{10,1... | collective-permute-start | bytes 61448 | tf_op jit(solution)/shard_map/ppermute | solution.py:17
  21.8 2.9 copy-start.3
  21.8 3.0 copy-start.5
  21.8 3.1 copy-start.10
  23.2 3.0 copy-start.4
  23.2 3.3 copy-start.6
  23.2 3.4 copy-start.7
  24.6 357.1 %all-gather.9.cloned.1.call-start = ((), (), s32[]{:S(2)}) async-start(), calls=%async_computation.1 | async-start | bytes 5898240 | tf_op jit(solution)/shard_map/all_gather | solution.py:94
  89.8 109.3 %copy-start.8 = (f32[2,2048]{1,0:T(2,128)S(1)}, f32[2,2048]{1,0:T(2,128)}, u32[]{:S(2)}) copy-start(f32[2,2048]{1,0:T(2,128)} %param.21) | copy-start | bytes 49156
  89.8 109.3 %copy-start.9 = (f32[2,2048]{1,0:T(2,128)S(1)}, f32[2,2048]{1,0:T(2,128)}, u32[]{:S(2)}) copy-start(f32[2,2048]{1,0:T(2,128)} %param.22) | copy-start | bytes 49156
  385.2 6.1 %copy-start.2 = (f32[4,40960]{1,0:T(4,128)S(1)}, f32[4,40960]{1,0:T(4,128)}, u32[]{:S(2)}) copy-start(f32[4,40960]{1,0:T(4,128)} %fusion.1) | copy-start | bytes 1966084
  385.2 12.2 %copy-start.1 = (f32[5,5]{1,0:T(8,128)S(1)}, f32[5,5]{1,0:T(8,128)}, u32[]{:S(2)}) copy-start(f32[5,5]{1,0:T(8,128)} %param.16) | copy-start | bytes 304
Sparse Core Ops, SparseCore 0:
  24.8 87.9 all-gather.6
  215.3 78.2 all-gather.8
where the time goes:
time: 405 us; the launch traced here: 404 us
  blocking collectives  208 us (51%)
  local copies, waits for them, and re-layouts  113 us (28%)
  other arithmetic  44.9 us (11%)
  matrix products  14.5 us (4%)
  between operations  13.9 us (3%)
  starting transfers between devices  9.47 us (2%)
    psum x2, blocking collectives, share_priors(): summed = lax.psum(masked, 'dom')  138 us
    gather x2, local copies, waits for them, and re-layouts, local_priors(): jnp.take(flat, points, axis=1).reshape(sample_total_size, nobs_count, 4)  70 us
    all_gather x2, blocking collectives, share_priors(): prior = lax.all_gather(summed, 'mem', axis=0, tiled=True)  69.7 us
    reduce_sum x2, other arithmetic, local_priors(): local_prior = jnp.sum(values * obs_weights[batch_index][None], axis=-1)  22.4 us
    unnamed x33, local copies, waits for them, and re-layouts  19.3 us
    select_n x2, other arithmetic, local_priors(): jnp.take(flat, points, axis=1).reshape(sample_total_size, nobs_count, 4)  12.4 us
    dot_general x2, matrix products, apply_update(): jnp.dot(own_columns.T, piece, precision=lax.Precision.HIGHEST, preferred_...  11.1 us
    sub x1, local copies, waits for them, and re-layouts, apply_update(): flat + product - jnp.sum(own_columns, axis=0)[:, None] * average[None]  11 us
  transfers between devices with their start and end apart: 6, of which 1 were waited for; matrix products, arithmetic and copies ran while one was open for 33% of the time, Pallas kernels for 0%

commit v1 on v0

--- a/solution.py
+++ b/solution.py
@@ -60,7 +60,8 @@
 
 def share_priors(local_prior, owned_mask):
     masked = jnp.where(owned_mask[None], local_prior, jnp.float32(0.0))
-    summed = lax.psum(masked, "dom")
+    parts = lax.all_gather(masked, "dom")
+    summed = jnp.sum(parts, axis=0)
     prior = lax.all_gather(summed, "mem", axis=0, tiled=True)
     return prior
 

time: 405 us -> 311 us (0.77)
  blocking collectives: 208 us -> 115 us
    psum x2 -> x0, blocking collectives: 138 us -> none  [share_priors(): summed = lax.psum(masked, 'dom')]
    all_gather x0 -> x2, blocking collectives: none -> 45.7 us  [share_priors(): parts = lax.all_gather(masked, 'dom')]
    unnamed x33 -> x31, local copies, waits for them, and re-layouts: 19.3 us -> 17.4 us
  transfers between devices with their start and end apart: 6 -> 6, of which waited for: 1 -> 1; matrix products, arithmetic and copies ran while one was open for 33% -> 43% of each run, Pallas kernels for 0% -> 0%
where the time goes in v1:
time: 311 us; the launch traced here: 310 us
  blocking collectives  115 us (37%)
  local copies, waits for them, and re-layouts  111 us (36%)
  other arithmetic  45.1 us (15%)
  matrix products  14.5 us (5%)
  between operations  13.9 us (4%)
  starting transfers between devices  9.47 us (3%)
    gather x2, local copies, waits for them, and re-layouts, local_priors(): jnp.take(flat, points, axis=1).reshape(sample_total_size, nobs_count, 4)  70 us
    all_gather x2, blocking collectives, share_priors(): prior = lax.all_gather(summed, 'mem', axis=0, tiled=True)  69.5 us
    all_gather x2, blocking collectives, share_priors(): parts = lax.all_gather(masked, 'dom')  45.7 us
    reduce_sum x2, other arithmetic, local_priors(): local_prior = jnp.sum(values * obs_weights[batch_index][None], axis=-1)  22.4 us
    unnamed x31, local copies, waits for them, and re-layouts  17.4 us
    select_n x2, other arithmetic, local_priors(): jnp.take(flat, points, axis=1).reshape(sample_total_size, nobs_count, 4)  12.4 us
    dot_general x2, matrix products, apply_update(): jnp.dot(own_columns.T, piece, precision=lax.Precision.HIGHEST, preferred_...  11.1 us
    sub x1, local copies, waits for them, and re-layouts, apply_update(): flat + product - jnp.sum(own_columns, axis=0)[:, None] * average[None]  11 us
  transfers between devices with their start and end apart: 6, of which 1 were waited for; matrix products, arithmetic and copies ran while one was open for 43% of the time, Pallas kernels for 0%

profile of v1, /device:TPU:0, one launch (start us, length us, event | category | flops | bytes accessed | tf_op | source)
XLA Modules:
  0.0 310.4 jit_solution(10799491245082273566)
XLA Ops:
  6.5 1.5 copy.48
  8.1 1.3 collective-permute-start
  9.4 3.0 collective-permute-start.1
  12.4 1.0 copy.41
  13.4 0.5 select_maximum_fusion.2
  14.0 1.4 fusion.4
  15.3 1.3 collective-permute-start.2
  16.6 3.8 %collective-permute-start.3 = (f32[4,5,1,256]{3,1,2,0:T(8,128)S(1)}, f32[4,5,1,256]{3,1,2,0:T(8,128)S(1)}, u32[]{:S(2)}, u32[]{:S(2)}) collective-permute-start(f32[4,5,1,256]{3,1,2,0:T(8,128)S(1)} %get-tuple-element.10), channel_id=1, source_target_pairs={{0,1},{1,2},{2,3},{3,4},{4,5},{5,6},{6,7},{7,8},{8,9},{9,10},{10,1... | collective-permute-start | bytes 61448 | tf_op jit(solution)/shard_map/ppermute | solution.py:17
  20.5 0.8 collective-permute-done.3
  21.3 0.5 select_maximum_fusion
  21.8 1.4 fusion.3
  23.2 0.2 copy.50
  23.4 1.2 reshape.273
  24.9 0.6 broadcast_add_fusion
  25.5 0.6 add.174
  26.2 0.4 copy.52
  26.7 0.4 copy.59
  27.1 10.0 %copy.51 = f32[4,40960]{0,1:T(8,128)} copy(f32[4,40960]{1,0:T(4,128)S(1)} %bitcast.64) | data formatting | bytes 1310720 | tf_op jit(solution)/shard_map/reshape | solution.py:91
  37.1 35.3 %gather_fusion = f32[8192,4]{1,0:T(8,128)} fusion(f32[4,40960]{0,1:T(8,128)} %copy.51, s32[8192]{0:T(1024)S(1)} %fusion.31), kind=kCustom, calls=%fused_computation.clone | custom fusion | bytes 294912 | tf_op jit(solution)/shard_map/jit(_take)/gather | solution.py:55
  72.4 6.2 %broadcast_select_fusion.1 = f32[8192,4]{1,0:T(8,128)S(1)} fusion(f32[8192,4]{1,0:T(8,128)} %gather_fusion, pred[8192]{0:T(1024)(128)(4,1)S(1)} %compare_and_fusion.1), kind=kLoop, calls=%fused_computation.11 | loop fusion | flops 32768 | bytes 270336 | tf_op jit(solution)/shard_map/jit(_take)/select_n | solution.py:55
  78.6 11.2 %multiply_reduce_fusion.1 = f32[4,2048]{0,1:T(8,128)S(1)} fusion(f32[4,2048,4]{0,2,1:T(4,128)S(1)} %bitcast.60, f32[2048,4]{1,0:T(8,128)S(1)} %copy.52), kind=kLoop, calls=%fused_computation.7 | loop fusion | flops 57344 | bytes 196608 | tf_op jit(solution)/shard_map/reduce_sum | solution.py:56
  89.8 0.3 bitcast_select_fusion.1
  90.2 0.3 copy.53
  90.5 26.8 %all_gather.20 = f32[16,4,2048]{2,1,0:T(4,128)S(1)} all-gather(f32[1,4,2048]{2,1,0:T(4,128)S(1)} %copy.53), channel_id=1, replica_groups=mesh['mem'=8,'dom'=16] {'dom'}, dimensions={0}, use_global_device_ids=true | all-gather | bytes 557056 | tf_op jit(solution)/shard_map/all_gather | solution.py:63
  117.4 34.9 %all-gather = f32[8,4,2048]{2,1,0:T(4,128)S(1)} all-gather(f32[1,4,2048]{2,1,0:T(4,128)S(1)} %bitcast.67), channel_id=1, replica_groups=mesh['mem'=8,'dom'=16] {'mem'}, dimensions={0}, use_global_device_ids=true | all-gather | bytes 294912 | tf_op jit(solution)/shard_map/all_gather | solution.py:65
  152.2 0.1 reshape.272
  152.5 0.4 fusion.17
  152.9 0.1 fusion.41
  153.1 3.5 %reduce_sum.118 = f32[40960]{0:T(1024)S(1)} reduce(f32[8,4,40960]{2,1,0:T(4,128)} %all-gather.7.cloned.1.call-done, f32[]{:T(128)} %constant.60.clone.1), dimensions={0,1}, to_apply=%region_5.7 | reduce | flops 1269760 | bytes 5406724 | tf_op jit(solution)/shard_map/reduce_sum | solution.py:99
  156.5 6.0 %reshape.274 = f32[32,40960]{1,0:T(8,128)} reshape(f32[8,4,40960]{2,1,0:T(4,128)} %all-gather.7.cloned.1.call-done) | data formatting | bytes 10485760
  162.6 6.0 %fusion.1 = f32[4,40960]{1,0:T(4,128)} fusion(f32[4,40960]{1,0:T(4,128)S(1)} %bitcast.65, f32[32,40960]{1,0:T(8,128)} %reshape.274, f32[40960]{0:T(1024)S(1)} %broadcast_multiply_fusion.1, f32[4]{0:T(128)S(1)} %fusion.41, f32[32,32]{0,1:T(8,128)S(1)} %fusion.17, s32[]{:T(128)S(6)} %select_n.70), kind=kOutput, calls=%fused_computation.5 | convolution fusion | flops 63406208 | bytes 6720004 | tf_op jit(solution)/shard_map/dot_general | solution.py:96
  168.6 0.6 add.185
  169.2 0.4 copy.56
  169.6 11.0 %copy.55 = f32[4,40960]{0,1:T(8,128)} copy(f32[4,40960]{1,0:T(4,128)} %fusion.1) | data formatting | bytes 1310720 | tf_op jit(solution)/shard_map/sub | solution.py:101
  180.6 34.7 %gather_fusion.1 = f32[8192,4]{1,0:T(8,128)} fusion(f32[4,40960]{0,1:T(8,128)} %copy.55, s32[8192]{0:T(1024)S(1)} %fusion.32), kind=kCustom, calls=%fused_computation.1.clone | custom fusion | bytes 294912 | tf_op jit(solution)/shard_map/jit(_take)/gather | solution.py:55
  215.3 6.2 %broadcast_select_fusion = f32[8192,4]{1,0:T(8,128)S(1)} fusion(f32[8192,4]{1,0:T(8,128)} %gather_fusion.1, pred[8192]{0:T(1024)(128)(4,1)S(1)} %compare_and_fusion), kind=kLoop, calls=%fused_computation.10 | loop fusion | flops 32768 | bytes 270336 | tf_op jit(solution)/shard_map/jit(_take)/select_n | solution.py:55
  221.5 11.2 %multiply_reduce_fusion = f32[4,2048]{0,1:T(8,128)S(1)} fusion(f32[4,2048,4]{0,2,1:T(4,128)S(1)} %bitcast.61, f32[2048,4]{1,0:T(8,128)S(1)} %copy.56), kind=kLoop, calls=%fused_computation.6 | loop fusion | flops 57344 | bytes 196608 | tf_op jit(solution)/shard_map/reduce_sum | solution.py:56
  232.8 0.3 bitcast_select_fusion
  233.1 0.3 copy.57
  233.4 18.9 %all_gather.23 = f32[16,4,2048]{2,1,0:T(4,128)S(1)} all-gather(f32[1,4,2048]{2,1,0:T(4,128)S(1)} %copy.57), channel_id=1, replica_groups=mesh['mem'=8,'dom'=16] {'dom'}, dimensions={0}, use_global_device_ids=true | all-gather | bytes 557056 | tf_op jit(solution)/shard_map/all_gather | solution.py:63
  252.5 34.6 %all-gather.2 = f32[8,4,2048]{2,1,0:T(4,128)S(1)} all-gather(f32[1,4,2048]{2,1,0:T(4,128)S(1)} %bitcast.68), channel_id=1, replica_groups=mesh['mem'=8,'dom'=16] {'mem'}, dimensions={0}, use_global_device_ids=true | all-gather | bytes 294912 | tf_op jit(solution)/shard_map/all_gather | solution.py:65
  287.1 0.1 reshape.276
  287.4 0.4 fusion.13
  287.8 0.1 fusion.42
  287.9 3.5 %reduce_sum.125 = f32[40960]{0:T(1024)S(1)} reduce(f32[8,4,40960]{2,1,0:T(4,128)} %all-gather.9.cloned.1.call-done, f32[]{:T(128)} %constant.60.clone.1), dimensions={0,1}, to_apply=%region_11.13 | reduce | flops 1269760 | bytes 5406724 | tf_op jit(solution)/shard_map/reduce_sum | solution.py:99
  291.4 6.1 %reshape.278 = f32[32,40960]{1,0:T(8,128)} reshape(f32[8,4,40960]{2,1,0:T(4,128)} %all-gather.9.cloned.1.call-done) | data formatting | bytes 10485760
  297.5 5.1 %fusion = f32[4,40960]{1,0:T(4,128)S(1)} fusion(f32[4,40960]{1,0:T(4,128)S(1)} %copy-done.2, f32[32,40960]{1,0:T(8,128)} %reshape.278, f32[40960]{0:T(1024)S(1)} %broadcast_multiply_fusion, f32[4]{0:T(128)S(1)} %fusion.42, f32[32,32]{0,1:T(8,128)S(1)} %fusion.13, s32[]{:T(128)S(6)} %select_n.70), kind=kOutput, calls=%fused_computation.3 | convolution fusion | flops 63406208 | bytes 6720004 | tf_op jit(solution)/shard_map/dot_general | solution.py:96
  302.6 1.0 copy.60
  (58 shorter events, 1.0 us)
Async XLA Ops:
  6.5 7.4 %copy-start = (f32[5,5]{1,0:T(8,128)S(1)}, f32[5,5]{1,0:T(8,128)}, u32[]{:S(2)}) copy-start(f32[5,5]{1,0:T(8,128)} %param.16) | copy-start | bytes 304
  6.5 146.5 %all-gather.7.cloned.1.call-start = ((), (), s32[]{:S(2)}) async-start(), calls=%async_computation | async-start | bytes 5898240 | tf_op jit(solution)/shard_map/all_gather | solution.py:95
  8.1 5.4 %collective-permute-start = (f32[4,5,1,256]{3,1,2,0:T(8,128)S(1)}, f32[4,5,1,256]{3,1,2,0:T(8,128)S(1)}, u32[]{:S(2)}, u32[]{:S(2)}) collective-permute-start(f32[4,5,1,256]{3,1,2,0:T(8,128)S(1)} %get-tuple-element.13), channel_id=1, source_target_pairs={{1,0},{2,1},{3,2},{4,3},{5,4},{6,5},{7,6},{8,7},{9,8},{10,9},{11,1... | collective-permute-start | bytes 61448 | tf_op jit(solution)/shard_map/ppermute | solution.py:19
  9.4 4.1 %collective-permute-start.1 = (f32[4,5,1,256]{3,1,2,0:T(8,128)S(1)}, f32[4,5,1,256]{3,1,2,0:T(8,128)S(1)}, u32[]{:S(2)}, u32[]{:S(2)}) collective-permute-start(f32[4,5,1,256]{3,1,2,0:T(8,128)S(1)} %get-tuple-element.12), channel_id=1, source_target_pairs={{0,1},{1,2},{2,3},{3,4},{4,5},{5,6},{6,7},{7,8},{8,9},{9,10},{10,1... | collective-permute-start | bytes 61448 | tf_op jit(solution)/shard_map/ppermute | solution.py:17
  15.3 5.1 %collective-permute-start.2 = (f32[4,5,1,256]{3,1,2,0:T(8,128)S(1)}, f32[4,5,1,256]{3,1,2,0:T(8,128)S(1)}, u32[]{:S(2)}, u32[]{:S(2)}) collective-permute-start(f32[4,5,1,256]{3,1,2,0:T(8,128)S(1)} %get-tuple-element.11), channel_id=1, source_target_pairs={{1,0},{2,1},{3,2},{4,3},{5,4},{6,5},{7,6},{8,7},{9,8},{10,9},{11,1... | collective-permute-start | bytes 61448 | tf_op jit(solution)/shard_map/ppermute | solution.py:19
  16.6 4.7 %collective-permute-start.3 = (f32[4,5,1,256]{3,1,2,0:T(8,128)S(1)}, f32[4,5,1,256]{3,1,2,0:T(8,128)S(1)}, u32[]{:S(2)}, u32[]{:S(2)}) collective-permute-start(f32[4,5,1,256]{3,1,2,0:T(8,128)S(1)} %get-tuple-element.10), channel_id=1, source_target_pairs={{0,1},{1,2},{2,3},{3,4},{4,5},{5,6},{6,7},{7,8},{8,9},{9,10},{10,1... | collective-permute-start | bytes 61448 | tf_op jit(solution)/shard_map/ppermute | solution.py:17
  21.8 2.9 copy-start.3
  21.8 3.0 copy-start.5
  21.8 3.1 copy-start.10
  23.2 3.0 copy-start.4
  23.2 3.3 %copy-start.6 = (s32[2,2048,1]{1,2,0:T(1,128)S(1)}, s32[2,2048,1]{1,2,0:T(1,128)}, u32[]{:S(2)}) copy-start(s32[2,2048,1]{1,2,0:T(1,128)} %param.17) | copy-start | bytes 49156
  23.2 3.4 %copy-start.7 = (f32[2,1,2048]{2,1,0:T(1,128)S(1)}, f32[2,1,2048]{2,1,0:T(1,128)}, u32[]{:S(2)}) copy-start(f32[2,1,2048]{2,1,0:T(1,128)} %param.23) | copy-start | bytes 49156
  24.6 263.3 %all-gather.9.cloned.1.call-start = ((), (), s32[]{:S(2)}) async-start(), calls=%async_computation.1 | async-start | bytes 5898240 | tf_op jit(solution)/shard_map/all_gather | solution.py:95
  89.8 62.6 %copy-start.8 = (f32[2,2048]{1,0:T(2,128)S(1)}, f32[2,2048]{1,0:T(2,128)}, u32[]{:S(2)}) copy-start(f32[2,2048]{1,0:T(2,128)} %param.21) | copy-start | bytes 49156
  89.8 62.6 %copy-start.9 = (f32[2,2048]{1,0:T(2,128)S(1)}, f32[2,2048]{1,0:T(2,128)}, u32[]{:S(2)}) copy-start(f32[2,2048]{1,0:T(2,128)} %param.22) | copy-start | bytes 49156
  291.4 6.1 %copy-start.2 = (f32[4,40960]{1,0:T(4,128)S(1)}, f32[4,40960]{1,0:T(4,128)}, u32[]{:S(2)}) copy-start(f32[4,40960]{1,0:T(4,128)} %fusion.1) | copy-start | bytes 1966084
  291.4 12.2 %copy-start.1 = (f32[5,5]{1,0:T(8,128)S(1)}, f32[5,5]{1,0:T(8,128)}, u32[]{:S(2)}) copy-start(f32[5,5]{1,0:T(8,128)} %param.16) | copy-start | bytes 304
Sparse Core Ops, SparseCore 0:
  24.8 87.9 all-gather.6
  168.7 78.3 all-gather.8
